TPU v7x, 32 devices: a whole 2x2x4 slice. The times are simulated.
32 devices in a mesh: tm: 4 (over x, core), space: 8 (over z, y).
Axes of the slice: x: 2, y: 2, z: 4, core: 2. Of those that a mesh axis runs over, the one named last changes fastest.
Arguments:
- cotangent: bfloat16 [16, 64, 8192], P('tm', 'space'), may hold values from -6 to 6
- saved_mix: bfloat16 [16, 64, 8192], P('tm', 'space'), may hold values from -6 to 6
- saved_pre: bfloat16 [16, 64, 8192], P('tm', 'space'), may hold values from -8 to 8
- kernel_one: bfloat16 [4, 3, 3, 64, 64], replicated, may hold values from -0.25 to 0.25
- kernel_two: bfloat16 [4, 3, 3, 64, 64], replicated, may hold values from -0.25 to 0.25
- ref_pairs: int32 [16, 2], replicated, may hold values from 0 to 15, as said below
- frame_level: int32 [16], replicated, may hold values from 0 to 4, as said below
Outputs:
- input_grad: float32 [16, 64, 8192], P('tm', 'space')
- weight_grad_one: float32 [4, 3, 3, 64, 64], replicated
- weight_grad_two: float32 [4, 3, 3, 64, 64], replicated
Inputs may be any that keep to these rules, and one draw needn't show every extreme that they name: Frame c was predicted from frames ref_pairs[c, 0] and ref_pairs[c, 1]; for a frame of level k >= 1 both have a level below k (at level 1 both name the level-0 frame); the level-0 frame names itself twice. `frame_level`: one frame has level 0 and 2**(k-1) frames have level k for k from 1 to 4; frames are stored in an order drawn from the seed.
All inputs are finite; a program needn't handle non-finite values.
Results may differ from a plain program's by a relative error of at most 0.006.
Values may be sent and summed in bfloat16 or wider, within the bound.
A program may use at most 64 MiB of HBM per device.

v0:
```python
import math
import jax
import jax.numpy as jnp
from jax import lax
from jax.sharding import PartitionSpec as P


def padded_2(cells, sides, width):
    for axis, dim in sides:
        count = lax.axis_size(axis)
        ends = count - 1
        head = lax.slice_in_dim(cells, 0, width, axis=dim)
        tail = lax.slice_in_dim(cells, cells.shape[dim] - width, cells.shape[dim], axis=dim)
        cells = jnp.concatenate(
            [
                lax.ppermute(tail, axis, [(i, (i + 1) % count) for i in range(ends)]),
                cells,
                lax.ppermute(head, axis, [((i + 1) % count, i) for i in range(ends)]),
            ],
            axis=dim,
        )
    return cells


def flipped(kernel):
    return jnp.transpose(kernel[::-1, ::-1], (0, 1, 3, 2))


def pair_kernel(kernel):
    blank = jnp.zeros_like(kernel[:, 0])
    row_blocks = []
    for in_part in range(4):
        col_blocks = []
        for out_half in range(2):
            col_tap = in_part - out_half
            col_blocks.append(kernel[:, col_tap] if 0 <= col_tap <= 2 else blank)
        row_blocks.append(jnp.concatenate(col_blocks, axis=-1))
    return jnp.concatenate(row_blocks, axis=1)


def pair_view(field, channels):
    col_count = field.shape[2] // channels
    grid = field.reshape(field.shape[0], field.shape[1], col_count, channels)
    grid = jnp.pad(grid, ((0, 0), (0, 0), (1, 1), (0, 0)))
    grid = grid.reshape(field.shape[0], field.shape[1], (col_count + 2) // 2, 2 * channels)
    return jnp.concatenate((grid[:, :, :-1], grid[:, :, 1:]), axis=-1)


def conv_taps(field, paired):
    channels = paired.shape[2] // 2
    windows = pair_view(field, channels)
    row_count = field.shape[1] - 2
    result = jnp.einsum(
        "nrjk,kc->nrjc", windows[:, 0:row_count], paired[0], preferred_element_type=jnp.float32
    )
    for row_tap in range(1, 3):
        result = result + jnp.einsum(
            "nrjk,kc->nrjc",
            windows[:, row_tap : row_tap + row_count],
            paired[row_tap],
            preferred_element_type=jnp.float32,
        )
    return result.reshape(field.shape[0], row_count, -1)


def correlate(field, cot, channels):
    windows = pair_view(field, channels)
    row_count = cot.shape[1]
    cot_pairs = cot.reshape(cot.shape[0], row_count, -1, 2 * channels)
    taps = []
    for row_tap in range(3):
        blocks = jnp.einsum(
            "nrjk,nrjc->nkc",
            windows[:, row_tap : row_tap + row_count],
            cot_pairs,
            preferred_element_type=jnp.float32,
        )
        row_taps = []
        for col_tap in range(3):
            first_part = blocks[:, col_tap * channels : (col_tap + 1) * channels, 0:channels]
            second_part = blocks[
                :, (col_tap + 1) * channels : (col_tap + 2) * channels, channels : 2 * channels
            ]
            row_taps.append(first_part + second_part)
        taps.append(jnp.stack(row_taps, axis=1))
    return jnp.stack(taps, axis=1)


def backprop(slot_cot, slot_slope, kernel_inner, kernel_outer):
    padded = padded_2(slot_cot, (("space", 1),), 1)
    slot_grad = (conv_taps(padded, kernel_inner) * slot_slope).astype(jnp.bfloat16)
    grad_padded = padded_2(slot_grad, (("space", 1),), 1)
    to_refs = conv_taps(grad_padded, kernel_outer).astype(jnp.bfloat16)
    return (slot_grad, to_refs)


def body_time(cotangent, saved_mix, saved_pre, kernel_one, kernel_two, ref_pairs, frame_level):
    frames_dev = cotangent.shape[0]
    row_count = cotangent.shape[1]
    channels = kernel_one.shape[-1]
    levels_all = kernel_one.shape[0]
    col_count = cotangent.shape[2] // channels
    first_frame = lax.axis_index("tm") * frames_dev
    local_ids = first_frame + jnp.arange(frames_dev, dtype=jnp.int32)
    local_level = lax.dynamic_slice_in_dim(frame_level, first_frame, frames_dev, 0)
    frame_count = ref_pairs.shape[0]
    all_frames = jnp.arange(frame_count, dtype=jnp.int32)
    preact = saved_pre.astype(jnp.float32)
    sigmoid_pre = jax.nn.sigmoid(preact)
    act_slope = sigmoid_pre * (1.0 + preact * (1.0 - sigmoid_pre))
    act_out = (preact * sigmoid_pre).astype(jnp.bfloat16)
    saved_rims = padded_2(jnp.stack((saved_mix, act_out)), (("space", 2),), 1)
    cot_total = cotangent.astype(jnp.float32)
    kept_grad = jnp.zeros_like(cotangent)
    for level_now in range(levels_all, 0, -1):
        active = local_level == level_now
        slot_count = min(frames_dev, 2 ** (level_now - 1))
        ranks = jnp.cumsum(active.astype(jnp.int32)) - 1
        picker = jnp.logical_and(
            ranks[None, :] == jnp.arange(slot_count, dtype=jnp.int32)[:, None], active[None, :]
        )
        picker_wide = picker.astype(jnp.float32)
        slot_cot = jnp.einsum(
            "sf,fx->sx",
            picker.astype(jnp.bfloat16),
            cot_total.astype(jnp.bfloat16).reshape(frames_dev, -1),
            preferred_element_type=jnp.float32,
        )
        slot_cot = slot_cot.astype(jnp.bfloat16).reshape(slot_count, row_count, -1)
        slot_slope = jnp.einsum(
            "sf,fx->sx",
            picker_wide,
            act_slope.reshape(frames_dev, -1),
            precision=lax.Precision.HIGHEST,
        ).reshape(slot_count, row_count, -1)
        slot_ids = jnp.sum(picker.astype(jnp.int32) * local_ids[None, :], axis=1)
        slot_ok = jnp.sum(picker.astype(jnp.int32), axis=1)
        kernel_inner = pair_kernel(flipped(kernel_two[level_now - 1]))
        kernel_outer = pair_kernel(flipped(kernel_one[level_now - 1]))
        slot_grad, to_refs = backprop(slot_cot, slot_slope, kernel_inner, kernel_outer)
        frame_grad = jnp.einsum(
            "sf,sx->fx",
            picker.astype(jnp.bfloat16),
            slot_grad.reshape(slot_grad.shape[0], -1),
            preferred_element_type=jnp.float32,
        )
        frame_grad = frame_grad.astype(jnp.bfloat16).reshape(kept_grad.shape)
        kept_grad = jnp.where(active[:, None, None], frame_grad, kept_grad)
        moved = lax.all_gather(to_refs, "tm", axis=0, tiled=True)
        sender_ids = lax.all_gather(slot_ids, "tm", axis=0, tiled=True)
        sender_ok = lax.all_gather(slot_ok, "tm", axis=0, tiled=True)
        matches = (sender_ids[:, None] == all_frames[None, :]).astype(jnp.int32)
        first_ref = jnp.sum(matches * ref_pairs[None, :, 0], axis=1)
        second_ref = jnp.sum(matches * ref_pairs[None, :, 1], axis=1)
        hits = (first_ref[:, None] == local_ids[None, :]).astype(jnp.float32) + (
            second_ref[:, None] == local_ids[None, :]
        ).astype(jnp.float32)
        weights = 0.5 * sender_ok[:, None].astype(jnp.float32) * hits
        added = jnp.einsum(
            "kf,kx->fx",
            weights.astype(jnp.bfloat16),
            moved.reshape(moved.shape[0], -1),
            preferred_element_type=jnp.float32,
        )
        cot_total = cot_total + added.reshape(cot_total.shape)
    final_cot = cot_total.astype(jnp.bfloat16)
    per_one = correlate(saved_rims[0], kept_grad, channels)
    per_two = correlate(saved_rims[1], final_cot, channels)
    level_hot = (
        local_level[:, None] == jnp.arange(1, levels_all + 1, dtype=jnp.int32)[None, :]
    ).astype(jnp.float32)
    scale = 1.0 / math.sqrt(row_count * lax.axis_size("space") * col_count)
    sum_one = scale * jnp.sum(level_hot[:, :, None, None, None, None] * per_one[:, None], axis=0)
    sum_two = scale * jnp.sum(level_hot[:, :, None, None, None, None] * per_two[:, None], axis=0)
    weight_one, weight_two = lax.psum((sum_one, sum_two), ("tm", "space"))
    return (cot_total, weight_one, weight_two)


def on_device(cotangent, saved_mix, saved_pre, kernel_one, kernel_two, ref_pairs, frame_level):
    return body_time(
        cotangent, saved_mix, saved_pre, kernel_one, kernel_two, ref_pairs, frame_level
    )


def solution(mesh):
    placed = (
        P("tm", "space", None),
        P("tm", "space", None),
        P("tm", "space", None),
        P(),
        P(),
        P(),
        P(),
    )
    return jax.shard_map(
        on_device,
        mesh=mesh,
        in_specs=placed,
        out_specs=(P("tm", "space", None), P(), P()),
        check_vma=False,
    )
```

profile of v0, /device:TPU:0, one launch (start us, length us, event | category | flops | bytes accessed | tf_op | source)
XLA Modules:
  0.0 384.8 jit_solution(5619695112859020218)
XLA Ops:
  13.1 4.9 %collective-permute-start = (bf16[4,1,8192]{2,0,1:T(4,128)(2,1)S(1)}, bf16[4,1,8192]{2,0,1:T(4,128)(2,1)S(1)}, u32[]{:S(2)}, u32[]{:S(2)}) collective-permute-start(bf16[4,1,8192]{2,0,1:T(4,128)(2,1)S(1)} %get-tuple-element.102), channel_id=1, source_target_pairs={{0,1},{1,2},{2,3},{3,4},{4,5},{5,6},{6,7},{8,9},{9,10},{10,11},{11... | collective-permute-start | bytes 196616 | tf_op jit(solution)/shard_map/ppermute | solution.py:16
  34.6 4.6 %collective-permute-start.2 = (bf16[4,1,8192]{2,0,1:T(4,128)(2,1)S(1)}, bf16[4,1,8192]{2,0,1:T(4,128)(2,1)S(1)}, u32[]{:S(2)}, u32[]{:S(2)}) collective-permute-start(bf16[4,1,8192]{2,0,1:T(4,128)(2,1)S(1)} %get-tuple-element.100), channel_id=1, source_target_pairs={{0,1},{1,2},{2,3},{3,4},{4,5},{5,6},{6,7},{8,9},{9,10},{10,11},{11... | collective-permute-start | bytes 196616 | tf_op jit(solution)/shard_map/ppermute | solution.py:16
  41.0 4.7 %collective-permute-done.3 = bf16[4,1,8192]{2,0,1:T(4,128)(2,1)S(1)} collective-permute-done((bf16[4,1,8192]{2,0,1:T(4,128)(2,1)S(1)}, bf16[4,1,8192]{2,0,1:T(4,128)(2,1)S(1)}, u32[]{:S(2)}, u32[]{:S(2)}) %collective-permute-start.3) | collective-permute-done | bytes 65568 | tf_op jit(solution)/shard_map/ppermute | solution.py:18
  55.1 5.7 %collective-permute-start.16 = (bf16[2,4,1,8192]{3,2,1,0:T(2,128)(2,1)}, bf16[2,4,1,8192]{3,2,1,0:T(2,128)(2,1)}, u32[]{:S(2)}, u32[]{:S(2)}) collective-permute-start(bf16[2,4,1,8192]{3,2,1,0:T(2,128)(2,1)} %get-tuple-element.54), channel_id=1, source_target_pairs={{0,1},{1,2},{2,3},{3,4},{4,5},{5,6},{6,7},{8,9},{9,10},{10,11},{11... | collective-permute-start | bytes 393224 | tf_op jit(solution)/shard_map/ppermute | solution.py:16
  69.0 5.7 %all-reduce.34 = (s32[16]{0:T(128)S(1)}, s32[16]{0:T(128)S(1)}, s32[16]{0:T(128)S(1)}, s32[16]{0:T(128)}, s32[8]{0:T(128)S(1)}, /*index=5*/s32[8]{0:T(128)}, s32[4]{0:T(128)S(1)}, s32[4]{0:T(128)}) all-reduce(s32[16]{0:T(128)S(1)} %dynamic-update-slice.3, s32[16]{0:T(128)S(1)} %dynamic-update-slice.1, ...), channel_id=1, replica_groups=mesh['tm'=4,'space'=8] {'tm'}, use_global_device_ids=true, to_apply=%add.29 | all-reduce | flops 88 | bytes 704
  78.1 5.5 %fusion.214 = (bf16[4,8,8192]{2,0,1:T(4,128)(2,1)S(1)}, f32[4,8,8192]{2,0,1:T(4,128)}) fusion(s32[16]{0:T(128)S(1)} %get-tuple-element.31, s32[16]{0:T(128)S(1)} %get-tuple-element.30, f32[16]{0:T(128)S(1)} %convert_multiply_fusion.5, s32[4]{0:T(128)S(1)} %get-tuple-element.160, bf16[4,8,8192]{2,1,0:T(8,128)(2,1)S(1)} %copy-done.31, ...), kind=kOutput, calls=%fused_computation.415 | convolution fusion | flops 9175488 | bytes 4194512 | tf_op jit(solution)/shard_map/kf,kx->fx/dot_general | solution.py:159
  84.2 3.4 collective-permute-start.4
  101.7 4.3 %collective-permute-start.6 = (bf16[4,1,8192]{2,0,1:T(4,128)(2,1)S(1)}, bf16[4,1,8192]{2,0,1:T(4,128)(2,1)S(1)}, u32[]{:S(2)}, u32[]{:S(2)}) collective-permute-start(bf16[4,1,8192]{2,0,1:T(4,128)(2,1)S(1)} %get-tuple-element.96), channel_id=1, source_target_pairs={{0,1},{1,2},{2,3},{3,4},{4,5},{5,6},{6,7},{8,9},{9,10},{10,11},{11... | collective-permute-start | bytes 196616 | tf_op jit(solution)/shard_map/ppermute | solution.py:16
  107.9 4.3 %collective-permute-done.7 = bf16[4,1,8192]{2,0,1:T(4,128)(2,1)S(1)} collective-permute-done((bf16[4,1,8192]{2,0,1:T(4,128)(2,1)S(1)}, bf16[4,1,8192]{2,0,1:T(4,128)(2,1)S(1)}, u32[]{:S(2)}, u32[]{:S(2)}) %collective-permute-start.7) | collective-permute-done | bytes 65568 | tf_op jit(solution)/shard_map/ppermute | solution.py:18
  124.9 2.4 fusion.143
  127.2 15.2 %all-gather.6.cloned.1.call-done = bf16[16,8,8192]{2,1,0:T(8,128)(2,1)} async-done(((bf16[4,8,8192]{2,1,0:T(8,128)(2,1)}), bf16[16,8,8192]{2,1,0:T(8,128)(2,1)}) %all-gather.6.cloned.1.call-update) | async-done | bytes 2097168 | tf_op jit(solution)/shard_map/all_gather | solution.py:149
  142.4 5.2 %fusion.215 = (bf16[4,8,8192]{2,0,1:T(4,128)(2,1)S(1)}, f32[4,8,8192]{2,0,1:T(4,128)}) fusion(f32[4,8,8192]{2,0,1:T(4,128)S(1)} %copy-done.14, s32[16]{0:T(128)S(1)} %get-tuple-element.32, s32[16]{0:T(128)S(1)} %get-tuple-element.29, f32[16]{0:T(128)S(1)} %convert_multiply_fusion.4, s32[4]{0:T(128)S(1)} %get-tuple-element.160, ...), kind=kOutput, calls=%fused_computation.416 | convolution fusion | flops 8913344 | bytes 4718800 | tf_op jit(solution)/shard_map/kf,kx->fx/dot_general | solution.py:159
  148.1 3.4 collective-permute-start.8
  154.5 2.7 collective-permute-done.9
  161.3 4.3 %collective-permute-start.10 = (bf16[2,1,8192]{2,0,1:T(2,128)(2,1)S(1)}, bf16[2,1,8192]{2,0,1:T(2,128)(2,1)S(1)}, u32[]{:S(2)}, u32[]{:S(2)}) collective-permute-start(bf16[2,1,8192]{2,0,1:T(2,128)(2,1)S(1)} %get-tuple-element.108), channel_id=1, source_target_pairs={{0,1},{1,2},{2,3},{3,4},{4,5},{5,6},{6,7},{8,9},{9,10},{10,11},{11... | collective-permute-start | bytes 98312 | tf_op jit(solution)/shard_map/ppermute | solution.py:16
  189.4 3.3 all-gather.8.cloned.1.call-done
  192.7 2.7 fusion.216
  196.0 3.4 collective-permute-start.12
  201.9 3.3 collective-permute-done.13
  211.1 4.3 %collective-permute-start.14 = (bf16[1,1,8192]{2,1,0:T(2,128)(2,1)S(1)}, bf16[1,1,8192]{2,1,0:T(2,128)(2,1)S(1)}, u32[]{:S(2)}, u32[]{:S(2)}) collective-permute-start(bf16[1,1,8192]{2,1,0:T(2,128)(2,1)S(1)} %get-tuple-element.140), channel_id=1, source_target_pairs={{0,1},{1,2},{2,3},{3,4},{4,5},{5,6},{6,7},{8,9},{9,10},{10,11},{11... | collective-permute-start | bytes 49160 | tf_op jit(solution)/shard_map/ppermute | solution.py:16
  218.5 2.7 collective-permute-done.15
  222.6 6.5 %all_gather.47 = bf16[4,8,8192]{2,1,0:T(8,128)(2,1)S(1)} all-gather(bf16[1,8,8192]{2,1,0:T(8,128)(2,1)S(1)} %convert_element_type.244), channel_id=1, replica_groups=mesh['tm'=4,'space'=8] {'tm'}, dimensions={0}, use_global_device_ids=true | all-gather | bytes 655360 | tf_op jit(solution)/shard_map/all_gather | solution.py:149
  240.2 134.1 %all-reduce.38.cloned.1.call-done = (f32[4,3,3,64,64]{4,3,2,1,0:T(8,128)}, f32[4,3,3,64,64]{4,3,2,1,0:T(8,128)}) async-done(((f32[4,3,3,64,64]{4,3,2,1,0:T(8,128)}, f32[4,3,3,64,64]{4,3,2,1,0:T(8,128)}), (f32[4,3,3,64,64]{4,3,2,1,0:T(8,128)}, f32[4,3,3,64,64]{4,3,2,1,0:T(8,128)})) %all-reduce.38.cloned.1.call-update) | async-done | bytes 1179664 | tf_op jit(solution)/shard_map/psum | solution.py:175
  374.3 2.5 copy.332
  (377 shorter events, 128.6 us)
Async XLA Ops:
  7.2 70.9 %all-gather.4.cloned.1.call-start = ((), (), s32[]{:S(2)}) async-start(), calls=%async_computation | async-start | bytes 2621440 | tf_op jit(solution)/shard_map/all_gather | solution.py:149
  9.3 56.3 %copy-start.39 = (pred[4]{0:T(512)(128)(4,1)}, pred[4]{0:T(512)(128)(4,1)S(1)}, u32[]{:S(2)}) copy-start(pred[4]{0:T(512)(128)(4,1)S(1)} %get-tuple-element.149) | copy-start | bytes 16
  13.1 12.7 %collective-permute-start = (bf16[4,1,8192]{2,0,1:T(4,128)(2,1)S(1)}, bf16[4,1,8192]{2,0,1:T(4,128)(2,1)S(1)}, u32[]{:S(2)}, u32[]{:S(2)}) collective-permute-start(bf16[4,1,8192]{2,0,1:T(4,128)(2,1)S(1)} %get-tuple-element.102), channel_id=1, source_target_pairs={{0,1},{1,2},{2,3},{3,4},{4,5},{5,6},{6,7},{8,9},{9,10},{10,11},{11... | collective-permute-start | bytes 196616 | tf_op jit(solution)/shard_map/ppermute | solution.py:16
  18.0 8.6 %collective-permute-start.1 = (bf16[4,1,8192]{2,0,1:T(4,128)(2,1)S(1)}, bf16[4,1,8192]{2,0,1:T(4,128)(2,1)S(1)}, u32[]{:S(2)}, u32[]{:S(2)}) collective-permute-start(bf16[4,1,8192]{2,0,1:T(4,128)(2,1)S(1)} %get-tuple-element.103), channel_id=1, source_target_pairs={{1,0},{2,1},{3,2},{4,3},{5,4},{6,5},{7,6},{9,8},{10,9},{11,10},{12... | collective-permute-start | bytes 196616 | tf_op jit(solution)/shard_map/ppermute | solution.py:18
  34.6 6.4 %collective-permute-start.2 = (bf16[4,1,8192]{2,0,1:T(4,128)(2,1)S(1)}, bf16[4,1,8192]{2,0,1:T(4,128)(2,1)S(1)}, u32[]{:S(2)}, u32[]{:S(2)}) collective-permute-start(bf16[4,1,8192]{2,0,1:T(4,128)(2,1)S(1)} %get-tuple-element.100), channel_id=1, source_target_pairs={{0,1},{1,2},{2,3},{3,4},{4,5},{5,6},{6,7},{8,9},{9,10},{10,11},{11... | collective-permute-start | bytes 196616 | tf_op jit(solution)/shard_map/ppermute | solution.py:16
  39.2 6.6 %collective-permute-start.3 = (bf16[4,1,8192]{2,0,1:T(4,128)(2,1)S(1)}, bf16[4,1,8192]{2,0,1:T(4,128)(2,1)S(1)}, u32[]{:S(2)}, u32[]{:S(2)}) collective-permute-start(bf16[4,1,8192]{2,0,1:T(4,128)(2,1)S(1)} %get-tuple-element.101), channel_id=1, source_target_pairs={{1,0},{2,1},{3,2},{4,3},{5,4},{6,5},{7,6},{9,8},{10,9},{11,10},{12... | collective-permute-start | bytes 196616 | tf_op jit(solution)/shard_map/ppermute | solution.py:18
  53.6 88.8 %all-gather.6.cloned.1.call-start = ((), (), s32[]{:S(2)}) async-start(), calls=%async_computation.1 | async-start | bytes 2621440 | tf_op jit(solution)/shard_map/all_gather | solution.py:149
  55.1 23.0 %copy-start.31 = (bf16[4,8,8192]{2,1,0:T(8,128)(2,1)S(1)}, bf16[4,8,8192]{2,1,0:T(8,128)(2,1)}, u32[]{:S(2)}) copy-start(bf16[4,8,8192]{2,1,0:T(8,128)(2,1)} %param.7) | copy-start | bytes 1572868
  55.1 112.0 %collective-permute-start.16 = (bf16[2,4,1,8192]{3,2,1,0:T(2,128)(2,1)}, bf16[2,4,1,8192]{3,2,1,0:T(2,128)(2,1)}, u32[]{:S(2)}, u32[]{:S(2)}) collective-permute-start(bf16[2,4,1,8192]{3,2,1,0:T(2,128)(2,1)} %get-tuple-element.54), channel_id=1, source_target_pairs={{0,1},{1,2},{2,3},{3,4},{4,5},{5,6},{6,7},{8,9},{9,10},{10,11},{11... | collective-permute-start | bytes 393224 | tf_op jit(solution)/shard_map/ppermute | solution.py:16
  60.8 106.3 %collective-permute-start.17 = (bf16[2,4,1,8192]{3,2,1,0:T(2,128)(2,1)}, bf16[2,4,1,8192]{3,2,1,0:T(2,128)(2,1)}, u32[]{:S(2)}, u32[]{:S(2)}) collective-permute-start(bf16[2,4,1,8192]{3,2,1,0:T(2,128)(2,1)} %get-tuple-element.55), channel_id=1, source_target_pairs={{1,0},{2,1},{3,2},{4,3},{5,4},{6,5},{7,6},{9,8},{10,9},{11,10},{12... | collective-permute-start | bytes 393224 | tf_op jit(solution)/shard_map/ppermute | solution.py:18
  84.2 6.7 %collective-permute-start.4 = (bf16[4,1,8192]{2,0,1:T(4,128)(2,1)S(1)}, bf16[4,1,8192]{2,0,1:T(4,128)(2,1)S(1)}, u32[]{:S(2)}, u32[]{:S(2)}) collective-permute-start(bf16[4,1,8192]{2,0,1:T(4,128)(2,1)S(1)} %get-tuple-element.98), channel_id=1, source_target_pairs={{0,1},{1,2},{2,3},{3,4},{4,5},{5,6},{6,7},{8,9},{9,10},{10,11},{11... | collective-permute-start | bytes 196616 | tf_op jit(solution)/shard_map/ppermute | solution.py:16
  87.6 6.2 %collective-permute-start.5 = (bf16[4,1,8192]{2,0,1:T(4,128)(2,1)S(1)}, bf16[4,1,8192]{2,0,1:T(4,128)(2,1)S(1)}, u32[]{:S(2)}, u32[]{:S(2)}) collective-permute-start(bf16[4,1,8192]{2,0,1:T(4,128)(2,1)S(1)} %get-tuple-element.99), channel_id=1, source_target_pairs={{1,0},{2,1},{3,2},{4,3},{5,4},{6,5},{7,6},{9,8},{10,9},{11,10},{12... | collective-permute-start | bytes 196616 | tf_op jit(solution)/shard_map/ppermute | solution.py:18
  101.7 6.2 %collective-permute-start.6 = (bf16[4,1,8192]{2,0,1:T(4,128)(2,1)S(1)}, bf16[4,1,8192]{2,0,1:T(4,128)(2,1)S(1)}, u32[]{:S(2)}, u32[]{:S(2)}) collective-permute-start(bf16[4,1,8192]{2,0,1:T(4,128)(2,1)S(1)} %get-tuple-element.96), channel_id=1, source_target_pairs={{0,1},{1,2},{2,3},{3,4},{4,5},{5,6},{6,7},{8,9},{9,10},{10,11},{11... | collective-permute-start | bytes 196616 | tf_op jit(solution)/shard_map/ppermute | solution.py:16
  106.0 6.2 %collective-permute-start.7 = (bf16[4,1,8192]{2,0,1:T(4,128)(2,1)S(1)}, bf16[4,1,8192]{2,0,1:T(4,128)(2,1)S(1)}, u32[]{:S(2)}, u32[]{:S(2)}) collective-permute-start(bf16[4,1,8192]{2,0,1:T(4,128)(2,1)S(1)} %get-tuple-element.97), channel_id=1, source_target_pairs={{1,0},{2,1},{3,2},{4,3},{5,4},{6,5},{7,6},{9,8},{10,9},{11,10},{12... | collective-permute-start | bytes 196616 | tf_op jit(solution)/shard_map/ppermute | solution.py:18
  120.5 72.2 %all-gather.8.cloned.1.call-start = ((), (), s32[]{:S(2)}) async-start(), calls=%async_computation.2 | async-start | bytes 1310720 | tf_op jit(solution)/shard_map/all_gather | solution.py:149
  148.1 6.3 %collective-permute-start.8 = (bf16[2,1,8192]{2,0,1:T(2,128)(2,1)S(1)}, bf16[2,1,8192]{2,0,1:T(2,128)(2,1)S(1)}, u32[]{:S(2)}, u32[]{:S(2)}) collective-permute-start(bf16[2,1,8192]{2,0,1:T(2,128)(2,1)S(1)} %get-tuple-element.110), channel_id=1, source_target_pairs={{0,1},{1,2},{2,3},{3,4},{4,5},{5,6},{6,7},{8,9},{9,10},{10,11},{11... | collective-permute-start | bytes 98312 | tf_op jit(solution)/shard_map/ppermute | solution.py:16
  151.5 5.8 %collective-permute-start.9 = (bf16[2,1,8192]{2,0,1:T(2,128)(2,1)S(1)}, bf16[2,1,8192]{2,0,1:T(2,128)(2,1)S(1)}, u32[]{:S(2)}, u32[]{:S(2)}) collective-permute-start(bf16[2,1,8192]{2,0,1:T(2,128)(2,1)S(1)} %get-tuple-element.111), channel_id=1, source_target_pairs={{1,0},{2,1},{3,2},{4,3},{5,4},{6,5},{7,6},{9,8},{10,9},{11,10},{12... | collective-permute-start | bytes 98312 | tf_op jit(solution)/shard_map/ppermute | solution.py:18
  161.3 7.8 %collective-permute-start.10 = (bf16[2,1,8192]{2,0,1:T(2,128)(2,1)S(1)}, bf16[2,1,8192]{2,0,1:T(2,128)(2,1)S(1)}, u32[]{:S(2)}, u32[]{:S(2)}) collective-permute-start(bf16[2,1,8192]{2,0,1:T(2,128)(2,1)S(1)} %get-tuple-element.108), channel_id=1, source_target_pairs={{0,1},{1,2},{2,3},{3,4},{4,5},{5,6},{6,7},{8,9},{9,10},{10,11},{11... | collective-permute-start | bytes 98312 | tf_op jit(solution)/shard_map/ppermute | solution.py:16
  165.6 5.8 %collective-permute-start.11 = (bf16[2,1,8192]{2,0,1:T(2,128)(2,1)S(1)}, bf16[2,1,8192]{2,0,1:T(2,128)(2,1)S(1)}, u32[]{:S(2)}, u32[]{:S(2)}) collective-permute-start(bf16[2,1,8192]{2,0,1:T(2,128)(2,1)S(1)} %get-tuple-element.109), channel_id=1, source_target_pairs={{1,0},{2,1},{3,2},{4,3},{5,4},{6,5},{7,6},{9,8},{10,9},{11,10},{12... | collective-permute-start | bytes 98312 | tf_op jit(solution)/shard_map/ppermute | solution.py:18
  176.8 197.5 %all-reduce.38.cloned.1.call-start = ((), (), s32[]{:S(2)}) async-start(), calls=%async_computation.3 | async-start | bytes 4718592 | tf_op jit(solution)/shard_map/psum | solution.py:175
  196.0 5.7 %collective-permute-start.12 = (bf16[1,1,8192]{2,1,0:T(2,128)(2,1)S(1)}, bf16[1,1,8192]{2,1,0:T(2,128)(2,1)S(1)}, u32[]{:S(2)}, u32[]{:S(2)}) collective-permute-start(bf16[1,1,8192]{2,1,0:T(2,128)(2,1)S(1)} %get-tuple-element.142), channel_id=1, source_target_pairs={{0,1},{1,2},{2,3},{3,4},{4,5},{5,6},{6,7},{8,9},{9,10},{10,11},{11... | collective-permute-start | bytes 49160 | tf_op jit(solution)/shard_map/ppermute | solution.py:16
  199.4 5.8 %collective-permute-start.13 = (bf16[1,1,8192]{2,1,0:T(2,128)(2,1)S(1)}, bf16[1,1,8192]{2,1,0:T(2,128)(2,1)S(1)}, u32[]{:S(2)}, u32[]{:S(2)}) collective-permute-start(bf16[1,1,8192]{2,1,0:T(2,128)(2,1)S(1)} %get-tuple-element.143), channel_id=1, source_target_pairs={{1,0},{2,1},{3,2},{4,3},{5,4},{6,5},{7,6},{9,8},{10,9},{11,10},{12... | collective-permute-start | bytes 49160 | tf_op jit(solution)/shard_map/ppermute | solution.py:18
  211.1 7.2 %collective-permute-start.14 = (bf16[1,1,8192]{2,1,0:T(2,128)(2,1)S(1)}, bf16[1,1,8192]{2,1,0:T(2,128)(2,1)S(1)}, u32[]{:S(2)}, u32[]{:S(2)}) collective-permute-start(bf16[1,1,8192]{2,1,0:T(2,128)(2,1)S(1)} %get-tuple-element.140), channel_id=1, source_target_pairs={{0,1},{1,2},{2,3},{3,4},{4,5},{5,6},{6,7},{8,9},{9,10},{10,11},{11... | collective-permute-start | bytes 49160 | tf_op jit(solution)/shard_map/ppermute | solution.py:16
  215.4 5.8 %collective-permute-start.15 = (bf16[1,1,8192]{2,1,0:T(2,128)(2,1)S(1)}, bf16[1,1,8192]{2,1,0:T(2,128)(2,1)S(1)}, u32[]{:S(2)}, u32[]{:S(2)}) collective-permute-start(bf16[1,1,8192]{2,1,0:T(2,128)(2,1)S(1)} %get-tuple-element.141), channel_id=1, source_target_pairs={{1,0},{2,1},{3,2},{4,3},{5,4},{6,5},{7,6},{9,8},{10,9},{11,10},{12... | collective-permute-start | bytes 49160 | tf_op jit(solution)/shard_map/ppermute | solution.py:18
  (60 other events, 303.9 us)
Sparse Core Ops, SparseCore 0:
  53.7 24.2 all-gather.3
  120.7 21.7 all-gather.5
  176.9 15.7 all-gather.7
  238.7 135.5 all-reduce.37
where the time goes:
time: 392 us; the launch traced here: 385 us
  waiting for transfers between devices  178 us (45%)
  local copies, waits for them, and re-layouts  60 us (15%)
  starting transfers between devices  51.1 us (13%)
  matrix products  39.3 us (10%)
  other arithmetic  27.3 us (7%)
  between operations  17.3 us (4%)
  blocking collectives  12.2 us (3%)
    psum x1, waiting for transfers between devices, body_time(): weight_one, weight_two = lax.psum((sum_one, sum_two), ('tm', 'space'))  134 us
    ppermute x9, starting transfers between devices, padded_2(): lax.ppermute(tail, axis, [(i, (i + 1) % count) for i in range(ends)])  38.1 us
    ppermute x9, waiting for transfers between devices, padded_2(): lax.ppermute(head, axis, [((i + 1) % count, i) for i in range(ends)])  21.9 us
    all_gather x3, waiting for transfers between devices, body_time(): moved = lax.all_gather(to_refs, 'tm', axis=0, tiled=True)  20.7 us
    unnamed x158, local copies, waits for them, and re-layouts  18.8 us
    dot_general x4, matrix products, body_time(): jnp.einsum('kf,kx->fx', weights.astype(jnp.bfloat16), moved.reshape(moved...  14.4 us
    ppermute x9, starting transfers between devices, padded_2(): lax.ppermute(head, axis, [((i + 1) % count, i) for i in range(ends)])  12.7 us
    dot_general x4, matrix products, body_time(): jnp.einsum('sf,fx->sx', picker_wide, act_slope.reshape(frames_dev, -1), p...  9.11 us
  transfers between devices with their start and end apart: 22, of which 13 were waited for; matrix products, arithmetic and copies ran while one was open for 19% of the time, Pallas kernels for 0%

commit v1 on v0

--- a/solution.py
+++ b/solution.py
@@ -172,7 +172,7 @@
     scale = 1.0 / math.sqrt(row_count * lax.axis_size("space") * col_count)
     sum_one = scale * jnp.sum(level_hot[:, :, None, None, None, None] * per_one[:, None], axis=0)
     sum_two = scale * jnp.sum(level_hot[:, :, None, None, None, None] * per_two[:, None], axis=0)
-    weight_one, weight_two = lax.psum((sum_one, sum_two), ("tm", "space"))
+    weight_one, weight_two = lax.psum(lax.psum((sum_one, sum_two), "space"), "tm")
     return (cot_total, weight_one, weight_two)
 
 

time: 392 us -> 424 us (1.082)
  waiting for transfers between devices: 178 us -> 206 us
    psum x1 -> x2, waiting for transfers between devices: 134 us -> 164 us  [the longest x1 108 us: body_time(): lax.psum((sum_one, sum_two), 'space')]
    unnamed x158 -> x162, local copies, waits for them, and re-layouts: 18.8 us -> 19.5 us
  transfers between devices with their start and end apart: 22 -> 23, of which waited for: 13 -> 14; matrix products, arithmetic and copies ran while one was open for 19% -> 18% of each run, Pallas kernels for 0% -> 0%
where the time goes in v1:
time: 424 us; the launch traced here: 417 us
  waiting for transfers between devices  206 us (49%)
  local copies, waits for them, and re-layouts  62.9 us (15%)
  starting transfers between devices  51.2 us (12%)
  matrix products  40.5 us (10%)
  other arithmetic  27.2 us (6%)
  between operations  17.2 us (4%)
  blocking collectives  12.2 us (3%)
    psum x1, waiting for transfers between devices, body_time(): lax.psum((sum_one, sum_two), 'space')  108 us
    psum x1, waiting for transfers between devices, body_time(): lax.psum(lax.psum((sum_one, sum_two), 'space'), 'tm')  55.5 us
    ppermute x9, starting transfers between devices, padded_2(): lax.ppermute(tail, axis, [(i, (i + 1) % count) for i in range(ends)])  38.1 us
    ppermute x9, waiting for transfers between devices, padded_2(): lax.ppermute(head, axis, [((i + 1) % count, i) for i in range(ends)])  21.9 us
    unnamed x162, local copies, waits for them, and re-layouts  19.5 us
    all_gather x3, waiting for transfers between devices, body_time(): moved = lax.all_gather(to_refs, 'tm', axis=0, tiled=True)  19 us
    dot_general x4, matrix products, body_time(): jnp.einsum('kf,kx->fx', weights.astype(jnp.bfloat16), moved.reshape(moved...  14.4 us
    ppermute x9, starting transfers between devices, padded_2(): lax.ppermute(head, axis, [((i + 1) % count, i) for i in range(ends)])  12.7 us
  transfers between devices with their start and end apart: 23, of which 14 were waited for; matrix products, arithmetic and copies ran while one was open for 18% of the time, Pallas kernels for 0%

profile of v1, /device:TPU:0, one launch (start us, length us, event | category | flops | bytes accessed | tf_op | source)
XLA Modules:
  0.0 416.7 jit_solution(3194860951852639385)
XLA Ops:
  13.0 4.9 %collective-permute-start = (bf16[4,1,8192]{2,0,1:T(4,128)(2,1)S(1)}, bf16[4,1,8192]{2,0,1:T(4,128)(2,1)S(1)}, u32[]{:S(2)}, u32[]{:S(2)}) collective-permute-start(bf16[4,1,8192]{2,0,1:T(4,128)(2,1)S(1)} %get-tuple-element.104), channel_id=1, source_target_pairs={{0,1},{1,2},{2,3},{3,4},{4,5},{5,6},{6,7},{8,9},{9,10},{10,11},{11... | collective-permute-start | bytes 196616 | tf_op jit(solution)/shard_map/ppermute | solution.py:16
  34.6 4.5 %collective-permute-start.2 = (bf16[4,1,8192]{2,0,1:T(4,128)(2,1)S(1)}, bf16[4,1,8192]{2,0,1:T(4,128)(2,1)S(1)}, u32[]{:S(2)}, u32[]{:S(2)}) collective-permute-start(bf16[4,1,8192]{2,0,1:T(4,128)(2,1)S(1)} %get-tuple-element.102), channel_id=1, source_target_pairs={{0,1},{1,2},{2,3},{3,4},{4,5},{5,6},{6,7},{8,9},{9,10},{10,11},{11... | collective-permute-start | bytes 196616 | tf_op jit(solution)/shard_map/ppermute | solution.py:16
  41.0 4.7 %collective-permute-done.3 = bf16[4,1,8192]{2,0,1:T(4,128)(2,1)S(1)} collective-permute-done((bf16[4,1,8192]{2,0,1:T(4,128)(2,1)S(1)}, bf16[4,1,8192]{2,0,1:T(4,128)(2,1)S(1)}, u32[]{:S(2)}, u32[]{:S(2)}) %collective-permute-start.3) | collective-permute-done | bytes 65568 | tf_op jit(solution)/shard_map/ppermute | solution.py:18
  55.1 5.7 %collective-permute-start.16 = (bf16[2,4,1,8192]{3,2,1,0:T(2,128)(2,1)}, bf16[2,4,1,8192]{3,2,1,0:T(2,128)(2,1)}, u32[]{:S(2)}, u32[]{:S(2)}) collective-permute-start(bf16[2,4,1,8192]{3,2,1,0:T(2,128)(2,1)} %get-tuple-element.56), channel_id=1, source_target_pairs={{0,1},{1,2},{2,3},{3,4},{4,5},{5,6},{6,7},{8,9},{9,10},{10,11},{11... | collective-permute-start | bytes 393224 | tf_op jit(solution)/shard_map/ppermute | solution.py:16
  68.7 5.6 %all-reduce.34 = (s32[16]{0:T(128)S(1)}, s32[16]{0:T(128)S(1)}, s32[16]{0:T(128)S(1)}, s32[16]{0:T(128)}, s32[8]{0:T(128)S(1)}, /*index=5*/s32[8]{0:T(128)}, s32[4]{0:T(128)S(1)}, s32[4]{0:T(128)}) all-reduce(s32[16]{0:T(128)S(1)} %dynamic-update-slice.3, s32[16]{0:T(128)S(1)} %dynamic-update-slice.1, ...), channel_id=1, replica_groups=mesh['tm'=4,'space'=8] {'tm'}, use_global_device_ids=true, to_apply=%add.29 | all-reduce | flops 88 | bytes 704
  75.4 2.6 all-gather.4.cloned.1.call-done
  78.0 5.5 %fusion.214 = (bf16[4,8,8192]{2,0,1:T(4,128)(2,1)S(1)}, f32[4,8,8192]{2,0,1:T(4,128)}) fusion(s32[16]{0:T(128)S(1)} %get-tuple-element.31, s32[16]{0:T(128)S(1)} %get-tuple-element.30, f32[16]{0:T(128)S(1)} %convert_multiply_fusion.5, s32[4]{0:T(128)S(1)} %get-tuple-element.162, bf16[4,8,8192]{2,1,0:T(8,128)(2,1)S(1)} %copy-done.31, ...), kind=kOutput, calls=%fused_computation.415 | convolution fusion | flops 9175488 | bytes 4194512 | tf_op jit(solution)/shard_map/kf,kx->fx/dot_general | solution.py:159
  84.2 3.4 collective-permute-start.4
  101.7 4.3 %collective-permute-start.6 = (bf16[4,1,8192]{2,0,1:T(4,128)(2,1)S(1)}, bf16[4,1,8192]{2,0,1:T(4,128)(2,1)S(1)}, u32[]{:S(2)}, u32[]{:S(2)}) collective-permute-start(bf16[4,1,8192]{2,0,1:T(4,128)(2,1)S(1)} %get-tuple-element.98), channel_id=1, source_target_pairs={{0,1},{1,2},{2,3},{3,4},{4,5},{5,6},{6,7},{8,9},{9,10},{10,11},{11... | collective-permute-start | bytes 196616 | tf_op jit(solution)/shard_map/ppermute | solution.py:16
  107.9 4.3 %collective-permute-done.7 = bf16[4,1,8192]{2,0,1:T(4,128)(2,1)S(1)} collective-permute-done((bf16[4,1,8192]{2,0,1:T(4,128)(2,1)S(1)}, bf16[4,1,8192]{2,0,1:T(4,128)(2,1)S(1)}, u32[]{:S(2)}, u32[]{:S(2)}) %collective-permute-start.7) | collective-permute-done | bytes 65568 | tf_op jit(solution)/shard_map/ppermute | solution.py:18
  127.2 15.2 %all-gather.6.cloned.1.call-done = bf16[16,8,8192]{2,1,0:T(8,128)(2,1)} async-done(((bf16[4,8,8192]{2,1,0:T(8,128)(2,1)}), bf16[16,8,8192]{2,1,0:T(8,128)(2,1)}) %all-gather.6.cloned.1.call-update) | async-done | bytes 2097168 | tf_op jit(solution)/shard_map/all_gather | solution.py:149
  142.4 5.2 %fusion.215 = (bf16[4,8,8192]{2,0,1:T(4,128)(2,1)S(1)}, f32[4,8,8192]{2,0,1:T(4,128)}) fusion(f32[4,8,8192]{2,0,1:T(4,128)S(1)} %copy-done.14, s32[16]{0:T(128)S(1)} %get-tuple-element.32, s32[16]{0:T(128)S(1)} %get-tuple-element.29, f32[16]{0:T(128)S(1)} %convert_multiply_fusion.4, s32[4]{0:T(128)S(1)} %get-tuple-element.162, ...), kind=kOutput, calls=%fused_computation.416 | convolution fusion | flops 8913344 | bytes 4718800 | tf_op jit(solution)/shard_map/kf,kx->fx/dot_general | solution.py:159
  148.1 3.4 collective-permute-start.8
  154.6 2.7 collective-permute-done.9
  161.3 4.3 %collective-permute-start.10 = (bf16[2,1,8192]{2,0,1:T(2,128)(2,1)S(1)}, bf16[2,1,8192]{2,0,1:T(2,128)(2,1)S(1)}, u32[]{:S(2)}, u32[]{:S(2)}) collective-permute-start(bf16[2,1,8192]{2,0,1:T(2,128)(2,1)S(1)} %get-tuple-element.110), channel_id=1, source_target_pairs={{0,1},{1,2},{2,3},{3,4},{4,5},{5,6},{6,7},{8,9},{9,10},{10,11},{11... | collective-permute-start | bytes 98312 | tf_op jit(solution)/shard_map/ppermute | solution.py:16
  192.8 2.7 fusion.216
  196.1 3.4 collective-permute-start.12
  202.0 3.3 collective-permute-done.13
  211.1 4.3 %collective-permute-start.14 = (bf16[1,1,8192]{2,1,0:T(2,128)(2,1)S(1)}, bf16[1,1,8192]{2,1,0:T(2,128)(2,1)S(1)}, u32[]{:S(2)}, u32[]{:S(2)}) collective-permute-start(bf16[1,1,8192]{2,1,0:T(2,128)(2,1)S(1)} %get-tuple-element.142), channel_id=1, source_target_pairs={{0,1},{1,2},{2,3},{3,4},{4,5},{5,6},{6,7},{8,9},{9,10},{10,11},{11... | collective-permute-start | bytes 49160 | tf_op jit(solution)/shard_map/ppermute | solution.py:16
  218.5 2.7 collective-permute-done.15
  222.6 6.5 %all_gather.47 = bf16[4,8,8192]{2,1,0:T(8,128)(2,1)S(1)} all-gather(bf16[1,8,8192]{2,1,0:T(8,128)(2,1)S(1)} %convert_element_type.244), channel_id=1, replica_groups=mesh['tm'=4,'space'=8] {'tm'}, dimensions={0}, use_global_device_ids=true | all-gather | bytes 655360 | tf_op jit(solution)/shard_map/all_gather | solution.py:149
  240.6 108.4 %all-reduce.40.cloned.1.call-done = (f32[4,3,3,64,64]{4,3,2,1,0:T(8,128)}, f32[4,3,3,64,64]{4,3,2,1,0:T(8,128)}) async-done(((f32[4,3,3,64,64]{4,3,2,1,0:T(8,128)}, f32[4,3,3,64,64]{4,3,2,1,0:T(8,128)}), (f32[4,3,3,64,64]{4,3,2,1,0:T(8,128)}, f32[4,3,3,64,64]{4,3,2,1,0:T(8,128)})) %all-reduce.40.cloned.1.call-update) | async-done | bytes 1179664 | tf_op jit(solution)/shard_map/psum | solution.py:175
  350.7 55.5 %all-reduce.42.cloned.1.call-done = (f32[4,3,3,64,64]{4,3,2,1,0:T(8,128)}, f32[4,3,3,64,64]{4,3,2,1,0:T(8,128)}) async-done(((f32[4,3,3,64,64]{4,3,2,1,0:T(8,128)}, f32[4,3,3,64,64]{4,3,2,1,0:T(8,128)}), (f32[4,3,3,64,64]{4,3,2,1,0:T(8,128)}, f32[4,3,3,64,64]{4,3,2,1,0:T(8,128)})) %all-reduce.42.cloned.1.call-update) | async-done | bytes 1179664 | tf_op jit(solution)/shard_map/psum | solution.py:175
  406.2 2.5 copy.334
  (384 shorter events, 133.9 us)
Async XLA Ops:
  7.2 70.9 %all-gather.4.cloned.1.call-start = ((), (), s32[]{:S(2)}) async-start(), calls=%async_computation | async-start | bytes 2621440 | tf_op jit(solution)/shard_map/all_gather | solution.py:149
  9.3 56.1 %copy-start.41 = (pred[4]{0:T(512)(128)(4,1)}, pred[4]{0:T(512)(128)(4,1)S(1)}, u32[]{:S(2)}) copy-start(pred[4]{0:T(512)(128)(4,1)S(1)} %get-tuple-element.151) | copy-start | bytes 16
  13.0 12.7 %collective-permute-start = (bf16[4,1,8192]{2,0,1:T(4,128)(2,1)S(1)}, bf16[4,1,8192]{2,0,1:T(4,128)(2,1)S(1)}, u32[]{:S(2)}, u32[]{:S(2)}) collective-permute-start(bf16[4,1,8192]{2,0,1:T(4,128)(2,1)S(1)} %get-tuple-element.104), channel_id=1, source_target_pairs={{0,1},{1,2},{2,3},{3,4},{4,5},{5,6},{6,7},{8,9},{9,10},{10,11},{11... | collective-permute-start | bytes 196616 | tf_op jit(solution)/shard_map/ppermute | solution.py:16
  18.0 8.6 %collective-permute-start.1 = (bf16[4,1,8192]{2,0,1:T(4,128)(2,1)S(1)}, bf16[4,1,8192]{2,0,1:T(4,128)(2,1)S(1)}, u32[]{:S(2)}, u32[]{:S(2)}) collective-permute-start(bf16[4,1,8192]{2,0,1:T(4,128)(2,1)S(1)} %get-tuple-element.105), channel_id=1, source_target_pairs={{1,0},{2,1},{3,2},{4,3},{5,4},{6,5},{7,6},{9,8},{10,9},{11,10},{12... | collective-permute-start | bytes 196616 | tf_op jit(solution)/shard_map/ppermute | solution.py:18
  34.6 6.4 %collective-permute-start.2 = (bf16[4,1,8192]{2,0,1:T(4,128)(2,1)S(1)}, bf16[4,1,8192]{2,0,1:T(4,128)(2,1)S(1)}, u32[]{:S(2)}, u32[]{:S(2)}) collective-permute-start(bf16[4,1,8192]{2,0,1:T(4,128)(2,1)S(1)} %get-tuple-element.102), channel_id=1, source_target_pairs={{0,1},{1,2},{2,3},{3,4},{4,5},{5,6},{6,7},{8,9},{9,10},{10,11},{11... | collective-permute-start | bytes 196616 | tf_op jit(solution)/shard_map/ppermute | solution.py:16
  39.2 6.6 %collective-permute-start.3 = (bf16[4,1,8192]{2,0,1:T(4,128)(2,1)S(1)}, bf16[4,1,8192]{2,0,1:T(4,128)(2,1)S(1)}, u32[]{:S(2)}, u32[]{:S(2)}) collective-permute-start(bf16[4,1,8192]{2,0,1:T(4,128)(2,1)S(1)} %get-tuple-element.103), channel_id=1, source_target_pairs={{1,0},{2,1},{3,2},{4,3},{5,4},{6,5},{7,6},{9,8},{10,9},{11,10},{12... | collective-permute-start | bytes 196616 | tf_op jit(solution)/shard_map/ppermute | solution.py:18
  53.6 88.8 %all-gather.6.cloned.1.call-start = ((), (), s32[]{:S(2)}) async-start(), calls=%async_computation.1 | async-start | bytes 2621440 | tf_op jit(solution)/shard_map/all_gather | solution.py:149
  55.1 112.0 %collective-permute-start.16 = (bf16[2,4,1,8192]{3,2,1,0:T(2,128)(2,1)}, bf16[2,4,1,8192]{3,2,1,0:T(2,128)(2,1)}, u32[]{:S(2)}, u32[]{:S(2)}) collective-permute-start(bf16[2,4,1,8192]{3,2,1,0:T(2,128)(2,1)} %get-tuple-element.56), channel_id=1, source_target_pairs={{0,1},{1,2},{2,3},{3,4},{4,5},{5,6},{6,7},{8,9},{9,10},{10,11},{11... | collective-permute-start | bytes 393224 | tf_op jit(solution)/shard_map/ppermute | solution.py:16
  60.7 106.4 %collective-permute-start.17 = (bf16[2,4,1,8192]{3,2,1,0:T(2,128)(2,1)}, bf16[2,4,1,8192]{3,2,1,0:T(2,128)(2,1)}, u32[]{:S(2)}, u32[]{:S(2)}) collective-permute-start(bf16[2,4,1,8192]{3,2,1,0:T(2,128)(2,1)} %get-tuple-element.57), channel_id=1, source_target_pairs={{1,0},{2,1},{3,2},{4,3},{5,4},{6,5},{7,6},{9,8},{10,9},{11,10},{12... | collective-permute-start | bytes 393224 | tf_op jit(solution)/shard_map/ppermute | solution.py:18
  84.2 6.7 %collective-permute-start.4 = (bf16[4,1,8192]{2,0,1:T(4,128)(2,1)S(1)}, bf16[4,1,8192]{2,0,1:T(4,128)(2,1)S(1)}, u32[]{:S(2)}, u32[]{:S(2)}) collective-permute-start(bf16[4,1,8192]{2,0,1:T(4,128)(2,1)S(1)} %get-tuple-element.100), channel_id=1, source_target_pairs={{0,1},{1,2},{2,3},{3,4},{4,5},{5,6},{6,7},{8,9},{9,10},{10,11},{11... | collective-permute-start | bytes 196616 | tf_op jit(solution)/shard_map/ppermute | solution.py:16
  87.6 6.2 %collective-permute-start.5 = (bf16[4,1,8192]{2,0,1:T(4,128)(2,1)S(1)}, bf16[4,1,8192]{2,0,1:T(4,128)(2,1)S(1)}, u32[]{:S(2)}, u32[]{:S(2)}) collective-permute-start(bf16[4,1,8192]{2,0,1:T(4,128)(2,1)S(1)} %get-tuple-element.101), channel_id=1, source_target_pairs={{1,0},{2,1},{3,2},{4,3},{5,4},{6,5},{7,6},{9,8},{10,9},{11,10},{12... | collective-permute-start | bytes 196616 | tf_op jit(solution)/shard_map/ppermute | solution.py:18
  101.7 6.2 %collective-permute-start.6 = (bf16[4,1,8192]{2,0,1:T(4,128)(2,1)S(1)}, bf16[4,1,8192]{2,0,1:T(4,128)(2,1)S(1)}, u32[]{:S(2)}, u32[]{:S(2)}) collective-permute-start(bf16[4,1,8192]{2,0,1:T(4,128)(2,1)S(1)} %get-tuple-element.98), channel_id=1, source_target_pairs={{0,1},{1,2},{2,3},{3,4},{4,5},{5,6},{6,7},{8,9},{9,10},{10,11},{11... | collective-permute-start | bytes 196616 | tf_op jit(solution)/shard_map/ppermute | solution.py:16
  106.0 6.2 %collective-permute-start.7 = (bf16[4,1,8192]{2,0,1:T(4,128)(2,1)S(1)}, bf16[4,1,8192]{2,0,1:T(4,128)(2,1)S(1)}, u32[]{:S(2)}, u32[]{:S(2)}) collective-permute-start(bf16[4,1,8192]{2,0,1:T(4,128)(2,1)S(1)} %get-tuple-element.99), channel_id=1, source_target_pairs={{1,0},{2,1},{3,2},{4,3},{5,4},{6,5},{7,6},{9,8},{10,9},{11,10},{12... | collective-permute-start | bytes 196616 | tf_op jit(solution)/shard_map/ppermute | solution.py:18
  120.6 72.2 %all-gather.8.cloned.1.call-start = ((), (), s32[]{:S(2)}) async-start(), calls=%async_computation.2 | async-start | bytes 1310720 | tf_op jit(solution)/shard_map/all_gather | solution.py:149
  148.1 6.4 %collective-permute-start.8 = (bf16[2,1,8192]{2,0,1:T(2,128)(2,1)S(1)}, bf16[2,1,8192]{2,0,1:T(2,128)(2,1)S(1)}, u32[]{:S(2)}, u32[]{:S(2)}) collective-permute-start(bf16[2,1,8192]{2,0,1:T(2,128)(2,1)S(1)} %get-tuple-element.112), channel_id=1, source_target_pairs={{0,1},{1,2},{2,3},{3,4},{4,5},{5,6},{6,7},{8,9},{9,10},{10,11},{11... | collective-permute-start | bytes 98312 | tf_op jit(solution)/shard_map/ppermute | solution.py:16
  151.5 5.8 %collective-permute-start.9 = (bf16[2,1,8192]{2,0,1:T(2,128)(2,1)S(1)}, bf16[2,1,8192]{2,0,1:T(2,128)(2,1)S(1)}, u32[]{:S(2)}, u32[]{:S(2)}) collective-permute-start(bf16[2,1,8192]{2,0,1:T(2,128)(2,1)S(1)} %get-tuple-element.113), channel_id=1, source_target_pairs={{1,0},{2,1},{3,2},{4,3},{5,4},{6,5},{7,6},{9,8},{10,9},{11,10},{12... | collective-permute-start | bytes 98312 | tf_op jit(solution)/shard_map/ppermute | solution.py:18
  161.3 7.9 %collective-permute-start.10 = (bf16[2,1,8192]{2,0,1:T(2,128)(2,1)S(1)}, bf16[2,1,8192]{2,0,1:T(2,128)(2,1)S(1)}, u32[]{:S(2)}, u32[]{:S(2)}) collective-permute-start(bf16[2,1,8192]{2,0,1:T(2,128)(2,1)S(1)} %get-tuple-element.110), channel_id=1, source_target_pairs={{0,1},{1,2},{2,3},{3,4},{4,5},{5,6},{6,7},{8,9},{9,10},{10,11},{11... | collective-permute-start | bytes 98312 | tf_op jit(solution)/shard_map/ppermute | solution.py:16
  165.6 5.8 %collective-permute-start.11 = (bf16[2,1,8192]{2,0,1:T(2,128)(2,1)S(1)}, bf16[2,1,8192]{2,0,1:T(2,128)(2,1)S(1)}, u32[]{:S(2)}, u32[]{:S(2)}) collective-permute-start(bf16[2,1,8192]{2,0,1:T(2,128)(2,1)S(1)} %get-tuple-element.111), channel_id=1, source_target_pairs={{1,0},{2,1},{3,2},{4,3},{5,4},{6,5},{7,6},{9,8},{10,9},{11,10},{12... | collective-permute-start | bytes 98312 | tf_op jit(solution)/shard_map/ppermute | solution.py:18
  176.8 172.2 %all-reduce.40.cloned.1.call-start = ((), (), s32[]{:S(2)}) async-start(), calls=%async_computation.3 | async-start | bytes 4718592 | tf_op jit(solution)/shard_map/psum | solution.py:175
  196.1 5.7 %collective-permute-start.12 = (bf16[1,1,8192]{2,1,0:T(2,128)(2,1)S(1)}, bf16[1,1,8192]{2,1,0:T(2,128)(2,1)S(1)}, u32[]{:S(2)}, u32[]{:S(2)}) collective-permute-start(bf16[1,1,8192]{2,1,0:T(2,128)(2,1)S(1)} %get-tuple-element.144), channel_id=1, source_target_pairs={{0,1},{1,2},{2,3},{3,4},{4,5},{5,6},{6,7},{8,9},{9,10},{10,11},{11... | collective-permute-start | bytes 49160 | tf_op jit(solution)/shard_map/ppermute | solution.py:16
  199.4 5.8 %collective-permute-start.13 = (bf16[1,1,8192]{2,1,0:T(2,128)(2,1)S(1)}, bf16[1,1,8192]{2,1,0:T(2,128)(2,1)S(1)}, u32[]{:S(2)}, u32[]{:S(2)}) collective-permute-start(bf16[1,1,8192]{2,1,0:T(2,128)(2,1)S(1)} %get-tuple-element.145), channel_id=1, source_target_pairs={{1,0},{2,1},{3,2},{4,3},{5,4},{6,5},{7,6},{9,8},{10,9},{11,10},{12... | collective-permute-start | bytes 49160 | tf_op jit(solution)/shard_map/ppermute | solution.py:18
  211.1 7.2 %collective-permute-start.14 = (bf16[1,1,8192]{2,1,0:T(2,128)(2,1)S(1)}, bf16[1,1,8192]{2,1,0:T(2,128)(2,1)S(1)}, u32[]{:S(2)}, u32[]{:S(2)}) collective-permute-start(bf16[1,1,8192]{2,1,0:T(2,128)(2,1)S(1)} %get-tuple-element.142), channel_id=1, source_target_pairs={{0,1},{1,2},{2,3},{3,4},{4,5},{5,6},{6,7},{8,9},{9,10},{10,11},{11... | collective-permute-start | bytes 49160 | tf_op jit(solution)/shard_map/ppermute | solution.py:16
  215.4 5.8 %collective-permute-start.15 = (bf16[1,1,8192]{2,1,0:T(2,128)(2,1)S(1)}, bf16[1,1,8192]{2,1,0:T(2,128)(2,1)S(1)}, u32[]{:S(2)}, u32[]{:S(2)}) collective-permute-start(bf16[1,1,8192]{2,1,0:T(2,128)(2,1)S(1)} %get-tuple-element.143), channel_id=1, source_target_pairs={{1,0},{2,1},{3,2},{4,3},{5,4},{6,5},{7,6},{9,8},{10,9},{11,10},{12... | collective-permute-start | bytes 49160 | tf_op jit(solution)/shard_map/ppermute | solution.py:18
  240.6 165.6 %all-reduce.42.cloned.1.call-start = ((), (), s32[]{:S(2)}) async-start(), calls=%async_computation.4 | async-start | bytes 4718592 | tf_op jit(solution)/shard_map/psum | solution.py:175
  (63 other events, 328.0 us)
Sparse Core Ops, SparseCore 0:
  53.7 24.2 all-gather.3
  120.7 21.6 all-gather.5
  177.0 15.7 all-gather.7
  240.7 108.3 all-reduce.39
  351.3 54.8 all-reduce.41
